TPU v7x, 32 devices: a whole 2x2x4 slice. The times are simulated.
32 devices in a mesh: rows: 8 (over z, y), rhs: 4 (over x, core).
Axes of the slice: x: 2, y: 2, z: 4, core: 2. Of those that a mesh axis runs over, the one named last changes fastest.
Arguments:
- right_sides: bfloat16 [64, 16384], P('rhs', 'rows'), may hold values from -6 to 6
- lower_inverse: bfloat16 [64, 256, 256], P('rows'), may hold values from -0.375 to 0.375
- lower_left: bfloat16 [64, 256, 32], P('rows'), may hold values from -1 to 1
- lower_right: bfloat16 [64, 256, 32], P('rows'), may hold values from -0.015625 to 0.015625
- upper_inverse: bfloat16 [64, 256, 256], P('rows'), may hold values from -0.375 to 0.375
- upper_left: bfloat16 [64, 256, 32], P('rows'), may hold values from -1 to 1
- upper_right: bfloat16 [64, 256, 32], P('rows'), may hold values from -0.015625 to 0.015625
- block_ranks: int32 [2, 64], P(None, 'rows'), may hold values from 8 to 32
Outputs:
- first_solve: float32 [64, 16384], P('rhs', 'rows')
- second_solve: float32 [64, 16384], P('rhs', 'rows')
All inputs are finite; a program needn't handle non-finite values.
Results may differ from a plain program's by a relative error of at most 0.0051.
Values may be sent and summed in bfloat16 or wider, within the bound.
A program may use at most 64 MiB of HBM per device.

v0:
```python
import jax
import jax.numpy as jnp
from jax import lax
from jax.sharding import PartitionSpec as P

highest = lax.Precision.HIGHEST


def compose_batched(earlier, later):
    return (
        jnp.matmul(earlier[0], later[0], precision=highest),
        jnp.matmul(earlier[1], later[0], precision=highest) + later[1],
    )


def prepare(coupled, masked, reverse):
    width = coupled.shape[2]
    kernels = jnp.eye(width, dtype=jnp.float32)[None] - jnp.einsum(
        "bjk,bjl->bkl", coupled, masked, precision=highest
    )

    def prepare_advance(running, inputs):
        kernel_row, coupled_row = inputs
        sensed = jnp.dot(running, coupled_row.T, precision=highest)
        return (jnp.dot(running, kernel_row, precision=highest), sensed)

    start = jnp.eye(width, dtype=jnp.float32)
    transfer, sensitivity = lax.scan(prepare_advance, start, (kernels, coupled), reverse=reverse)
    return (transfer, sensitivity)


def local_pass(pushed, coupled, masked, start, reverse):

    def local_advance(state, inputs):
        pushed_row, coupled_row, masked_row = inputs
        solved = pushed_row - jnp.dot(state, coupled_row.T, precision=highest)
        state = state + jnp.dot(solved, masked_row, precision=highest)
        return (state, solved)

    return lax.scan(local_advance, start, (pushed, coupled, masked), reverse=reverse)


def fold_collected(maps, offsets, reverse):
    position = lax.axis_index("rows")
    count = maps.shape[0]
    order = jnp.arange(count, dtype=jnp.int32)
    include = order > position if reverse else order < position
    identity = jnp.eye(maps.shape[1], dtype=jnp.float32)
    maps = jnp.where(include[:, None, None], maps, identity[None])
    offsets = jnp.where(include[:, None, None], offsets, jnp.zeros_like(offsets))
    if reverse:
        maps = maps[::-1]
        offsets = offsets[::-1]
    folded = lax.associative_scan(compose_batched, (maps, offsets))
    return folded[1][-1]


def carry_in(transfer, offset, reverse):
    if reverse:
        maps, offsets = (
            lax.all_gather(transfer[None], "rows", axis=0, tiled=True),
            lax.all_gather(offset[None], "rows", axis=0, tiled=True),
        )
    else:
        maps, offsets = (
            lax.all_gather(transfer[None], "rows", axis=0, tiled=True),
            lax.all_gather(offset[None], "rows", axis=0, tiled=True),
        )
    return fold_collected(maps, offsets, reverse)


def apply_solve(values, inverse, coupled, masked, transfer, reverse):
    rows_rhs = values.shape[0]
    blocks, order_block = (inverse.shape[0], inverse.shape[1])
    width = coupled.shape[2]
    blocked = values.reshape(rows_rhs, blocks, order_block)
    pushed = jnp.einsum("rbk,bjk->brj", blocked, inverse, preferred_element_type=jnp.float32)
    empty_state = jnp.zeros((rows_rhs, width), jnp.float32)
    offset, zero_state = local_pass(pushed, coupled, masked, empty_state, reverse)
    incoming = carry_in(transfer, offset, reverse)
    _, solved = local_pass(pushed, coupled, masked, incoming, reverse)
    return jnp.transpose(solved, (1, 0, 2)).reshape(rows_rhs, blocks * order_block)


def rank_masked(right_factor, ranks_row):
    columns = jnp.arange(right_factor.shape[2], dtype=jnp.int32)
    rank_mask = (columns[None, :] < ranks_row[:, None]).astype(jnp.float32)
    return right_factor.astype(jnp.float32) * rank_mask[:, None, :]


def coupled_product(inverse, left_factor):
    return jnp.einsum(
        "bij,bjk->bik", inverse, left_factor, preferred_element_type=jnp.float32
    ).astype(jnp.bfloat16)


def local(
    right_sides,
    lower_inverse,
    lower_left,
    lower_right,
    upper_inverse,
    upper_left,
    upper_right,
    block_ranks,
):
    lower_full = coupled_product(lower_inverse, lower_left)
    upper_full = coupled_product(upper_inverse, upper_left)
    lower_coupled = lower_full.astype(jnp.float32)
    upper_coupled = upper_full.astype(jnp.float32)
    lower_masked = rank_masked(lower_right, block_ranks[0])
    upper_masked = rank_masked(upper_right, block_ranks[1])
    lower_transfer, lower_sense = prepare(lower_coupled, lower_masked, False)
    upper_transfer, upper_sense = prepare(upper_coupled, upper_masked, True)
    forward = apply_solve(
        right_sides, lower_inverse, lower_coupled, lower_masked, lower_transfer, False
    )
    first_solve = apply_solve(
        forward.astype(jnp.bfloat16),
        upper_inverse,
        upper_coupled,
        upper_masked,
        upper_transfer,
        True,
    )
    forward_again = apply_solve(
        first_solve.astype(jnp.bfloat16),
        lower_inverse,
        lower_coupled,
        lower_masked,
        lower_transfer,
        False,
    )
    second_solve = apply_solve(
        forward_again.astype(jnp.bfloat16),
        upper_inverse,
        upper_coupled,
        upper_masked,
        upper_transfer,
        True,
    )
    return (first_solve, second_solve)


def solution(mesh):
    placed = (
        P("rhs", "rows"),
        P("rows", None, None),
        P("rows", None, None),
        P("rows", None, None),
        P("rows", None, None),
        P("rows", None, None),
        P("rows", None, None),
        P(None, "rows"),
    )
    return jax.shard_map(
        local,
        mesh=mesh,
        in_specs=placed,
        out_specs=(P("rhs", "rows"), P("rhs", "rows")),
        check_vma=False,
    )
```

profile of v0, /device:TPU:0, one launch (start us, length us, event | category | flops | bytes accessed | tf_op | source)
XLA Modules:
  0.0 325.1 jit_solution(10656291714458815830)
XLA Ops:
  2.7 1.8 convolution_convert_fusion
  5.1 2.0 while.134
  7.2 32.3 %all-gather.3 = f32[256,32]{1,0:T(8,128)S(1)} all-gather(f32[32,32]{1,0:T(8,128)S(1)} %copy.38), channel_id=5, replica_groups=mesh['rows'=8,'rhs'=4] {'rows'}, dimensions={0}, use_global_device_ids=true | all-gather | bytes 36864 | tf_op jit(solution)/shard_map/all_gather | solution.py:61
  41.4 2.0 while.132
  43.5 30.5 %all-gather.1 = f32[256,32]{1,0:T(8,128)S(1)} all-gather(f32[32,32]{1,0:T(8,128)S(1)} %copy.33), channel_id=3, replica_groups=mesh['rows'=8,'rhs'=4] {'rows'}, dimensions={0}, use_global_device_ids=true | all-gather | bytes 36864 | tf_op jit(solution)/shard_map/all_gather | solution.py:66
  75.1 1.9 fusion.87
  77.0 9.2 %while.138 = (s32[]{:T(128)}, f32[16,32]{1,0:T(8,128)S(1)}, f32[8,16,256]{2,1,0:T(8,128)}, f32[8,256,32]{2,1,0:T(8,128)S(1)}, f32[8,256,32]{2,1,0:T(8,128)S(1)}, /*index=5*/s32[]{:T(128)}, s32[]{:T(128)}) while((s32[]{:T(128)}, f32[16,32]{1,0:T(8,128)S(1)}, f32[8,16,256]{2,1,0:T(8,128)}, f32[8,256,32]{2,1,0:T(8,128)S(1)}, ...), condition=%wide.region_1.2_spmd.clone, body=%wide.region_0.1_spmd.clone.sunk | while | flops 3151363 | bytes 330844 | solution.py:40
  86.2 30.7 %all-gather = f32[128,32]{1,0:T(8,128)S(1)} all-gather(f32[16,32]{1,0:T(8,128)S(1)} %get-tuple-element.652), channel_id=2, replica_groups=mesh['rows'=8,'rhs'=4] {'rows'}, dimensions={0}, use_global_device_ids=true | all-gather | bytes 18432 | tf_op jit(solution)/shard_map/all_gather | solution.py:67
  119.6 1.9 pad.79
  124.3 1.4 add.292
  125.7 3.2 pad.193
  130.3 13.9 %while.133 = (s32[]{:T(128)}, f32[16,32]{1,0:T(8,128)S(1)}, bf16[8,16,256]{2,1,0:T(8,128)(2,1)}, f32[8,16,256]{2,1,0:T(8,128)}, f32[8,256,32]{2,1,0:T(8,128)S(1)}, /*index=5*/f32[8,256,32]{2,1,0:T(8,128)S(1)}, s32[]{:T(128)}) while((s32[]{:T(128)}, f32[16,32]{1,0:T(8,128)S(1)}, bf16[8,16,256]{2,1,0:T(8,128)(2,1)}, f32[8,16,256]{2,1,0:T(8,128)}, ...), condition=%wide.region_5.6_spmd, body=%wide.region_4.5_spmd.sunk | while | flops 3150338 | bytes 347217 | solution.py:40
  130.3 1.5 bitcast_dynamic-update-slice_fusion.8
  132.0 1.5 bitcast_dynamic-update-slice_fusion.8
  133.8 1.5 bitcast_dynamic-update-slice_fusion.8
  135.5 1.5 bitcast_dynamic-update-slice_fusion.8
  137.3 1.5 bitcast_dynamic-update-slice_fusion.8
  139.0 1.5 bitcast_dynamic-update-slice_fusion.8
  140.7 1.5 bitcast_dynamic-update-slice_fusion.8
  142.5 1.5 bitcast_dynamic-update-slice_fusion.8
  144.2 2.7 fusion.92
  149.3 10.8 %while.139 = (s32[]{:T(128)}, f32[16,32]{1,0:T(8,128)S(1)}, f32[8,16,256]{2,1,0:T(8,128)}, f32[8,256,32]{2,1,0:T(8,128)}, f32[8,256,32]{2,1,0:T(8,128)S(1)}, /*index=5*/s32[]{:T(128)}, s32[]{:T(128)}, s32[]{:T(128)}) while((s32[]{:T(128)}, f32[16,32]{1,0:T(8,128)S(1)}, f32[8,16,256]{2,1,0:T(8,128)}, f32[8,256,32]{2,1,0:T(8,128)}, ...), condition=%wide.region_7.8_spmd.clone, body=%wide.region_6.7_spmd.clone.sunk | while | flops 3151364 | bytes 325231 | solution.py:40
  160.0 30.5 %all-gather.2 = f32[128,32]{1,0:T(8,128)S(1)} all-gather(f32[16,32]{1,0:T(8,128)S(1)} %get-tuple-element.655), channel_id=4, replica_groups=mesh['rows'=8,'rhs'=4] {'rows'}, dimensions={0}, use_global_device_ids=true | all-gather | bytes 18432 | tf_op jit(solution)/shard_map/all_gather | solution.py:62
  196.1 10.8 %while.135 = (s32[]{:T(128)}, f32[16,32]{1,0:T(8,128)S(1)}, f32[8,16,256]{2,1,0:T(8,128)S(1)}, f32[8,16,256]{2,1,0:T(8,128)}, f32[8,256,32]{2,1,0:T(8,128)}, /*i...) while((s32[]{:T(128)}, f32[16,32]{1,0:T(8,128)S(1)}, f32[8,16,256]{2,1,0:T(8,128)S(1)}, ...), condition=%wide.region_11.12_spmd, body=%wide.region_10.11_spmd.sunk | while | flops 3150339 | bytes 347237 | solution.py:40
  208.0 10.7 %while.140 = (s32[]{:T(128)}, f32[16,32]{1,0:T(8,128)S(1)}, f32[8,16,256]{2,1,0:T(8,128)}, f32[8,256,32]{2,1,0:T(8,128)}, f32[8,256,32]{2,1,0:T(8,128)S(1)}, /*index=5*/s32[]{:T(128)}, s32[]{:T(128)}) while((s32[]{:T(128)}, f32[16,32]{1,0:T(8,128)S(1)}, f32[8,16,256]{2,1,0:T(8,128)}, f32[8,256,32]{2,1,0:T(8,128)}, ...), condition=%wide.region_13.14_spmd.clone, body=%wide.region_12.13_spmd.clone.sunk | while | flops 3151363 | bytes 324700 | solution.py:40
  218.7 30.5 %all-gather.4 = f32[128,32]{1,0:T(8,128)S(1)} all-gather(f32[16,32]{1,0:T(8,128)S(1)} %get-tuple-element.658), channel_id=6, replica_groups=mesh['rows'=8,'rhs'=4] {'rows'}, dimensions={0}, use_global_device_ids=true | all-gather | bytes 18432 | tf_op jit(solution)/shard_map/all_gather | solution.py:67
  254.1 1.8 pad.197
  256.6 10.8 %while.136 = (s32[]{:T(128)}, f32[16,32]{1,0:T(8,128)S(1)}, bf16[8,16,256]{2,1,0:T(8,128)(2,1)S(1)}, f32[8,16,256]{2,1,0:T(8,128)}, f32[8,256,32]{2,1,0:T(8,128)}, /*index=5*/f32[8,256,32]{2,1,0:T(8,128)S(1)}, s32[]{:T(128)}) while((s32[]{:T(128)}, f32[16,32]{1,0:T(8,128)S(1)}, bf16[8,16,256]{2,1,0:T(8,128)(2,1)S(1)}, ...), condition=%wide.region_15.16_spmd, body=%wide.region_14.15_spmd.sunk | while | flops 3150338 | bytes 347217 | solution.py:40
  267.4 1.6 fusion.90
  269.0 10.7 %while.141 = (s32[]{:T(128)}, f32[16,32]{1,0:T(8,128)S(1)}, f32[8,16,256]{2,1,0:T(8,128)S(1)}, f32[8,256,32]{2,1,0:T(8,128)}, f32[8,256,32]{2,1,0:T(8,128)S(1)}, /*index=5*/s32[]{:T(128)}, s32[]{:T(128)}, s32[]{:T(128)}) while((s32[]{:T(128)}, f32[16,32]{1,0:T(8,128)S(1)}, f32[8,16,256]{2,1,0:T(8,128)S(1)}, ...), condition=%wide.region_17.18_spmd.clone, body=%wide.region_16.17_spmd.clone.sunk | while | flops 3151364 | bytes 325231 | solution.py:40
  279.8 30.5 %all-gather.5 = f32[128,32]{1,0:T(8,128)S(1)} all-gather(f32[16,32]{1,0:T(8,128)S(1)} %get-tuple-element.660), channel_id=7, replica_groups=mesh['rows'=8,'rhs'=4] {'rows'}, dimensions={0}, use_global_device_ids=true | all-gather | bytes 18432 | tf_op jit(solution)/shard_map/all_gather | solution.py:62
  313.1 10.7 %while.137 = (s32[]{:T(128)}, f32[16,32]{1,0:T(8,128)S(1)}, f32[8,16,256]{2,1,0:T(8,128)S(1)}, f32[8,16,256]{2,1,0:T(8,128)S(1)}, f32[8,256,32]{2,1,0:T(8,128)},...) while((s32[]{:T(128)}, f32[16,32]{1,0:T(8,128)S(1)}, f32[8,16,256]{2,1,0:T(8,128)S(1)}, ...), condition=%wide.region_19.20_spmd, body=%wide.region_18.19_spmd.sunk | while | flops 3150339 | bytes 347237 | solution.py:40
  (309 shorter events, 107.3 us)
Async XLA Ops:
  0.6 39.2 %copy-start = (bf16[8,256,256]{2,1,0:T(8,128)(2,1)S(1)}, bf16[8,256,256]{2,1,0:T(8,128)(2,1)}, u32[]{:S(2)}) copy-start(bf16[8,256,256]{2,1,0:T(8,128)(2,1)} %param.29) | copy-start | bytes 3145732
  0.7 0.8 copy-start.29
  1.5 3.1 copy-start.22
  1.5 1.2 copy-start.14
  2.7 1.9 copy-start.2
  7.1 32.4 %copy-start.15 = (bf16[8,256,32]{1,2,0:T(8,128)(2,1)S(1)}, bf16[8,256,32]{1,2,0:T(8,128)(2,1)}, u32[]{:S(2)}) copy-start(bf16[8,256,32]{1,2,0:T(8,128)(2,1)} %param.31) | copy-start | bytes 393220
  39.6 0.9 copy-start.16
  74.0 42.9 %copy-start.27 = (pred[8]{0:T(512)(128)(4,1)}, pred[8]{0:T(512)(128)(4,1)S(1)}, u32[]{:S(2)}) copy-start(pred[8]{0:T(512)(128)(4,1)S(1)} %iota_compare_fusion.3) | copy-start | bytes 28
  74.0 0.7 copy-start.24
  86.2 30.8 %copy-start.3 = (f32[8,32,32]{2,1,0:T(8,128)S(1)}, f32[8,32,32]{2,1,0:T(8,128)}, u32[]{:S(2)}) copy-start(f32[8,32,32]{2,1,0:T(8,128)} %get-tuple-element.936) | copy-start | bytes 98308
  117.1 0.6 copy-start.21
  117.8 0.6 copy-start.4
  122.4 0.7 slice-start.2
  129.6 0.7 copy-start.8
  144.2 2.7 copy-start.1
  144.2 2.7 copy-start.23
  190.6 0.7 copy-start.25
  192.1 0.8 copy-start.17
  192.9 2.2 copy-start.6
  193.2 0.6 copy-start.12
  194.4 0.8 copy-start.18
  195.3 0.7 slice-start
  249.3 0.7 copy-start.28
  250.0 0.8 copy-start.5
  250.9 0.6 copy-start.19
  250.9 0.7 copy-start.11
  251.7 0.8 copy-start.20
  253.3 0.7 slice-start.1
  254.1 2.5 copy-start.9
  310.3 0.7 copy-start.26
  311.1 0.8 copy-start.7
  311.9 0.7 copy-start.13
  (1 other events, 0.6 us)
where the time goes:
time: 329 us; the launch traced here: 325 us
  blocking collectives  185 us (56%)
  matrix products  104 us (32%)
  local copies, waits for them, and re-layouts  25.2 us (8%)
  other arithmetic  6.41 us (2%)
    all_gather x4, blocking collectives, carry_in(): lax.all_gather(offset[None], 'rows', axis=0, tiled=True)  122 us
    dot_general x64, matrix products, local_advance(): solved = pushed_row - jnp.dot(state, coupled_row.T, precision=highest)  73.3 us
    all_gather x2, blocking collectives, carry_in(): lax.all_gather(transfer[None], 'rows', axis=0, tiled=True)  62.8 us
    unnamed x70, local copies, waits for them, and re-layouts  17.5 us
    dot_general x64, matrix products, local_advance(): state = state + jnp.dot(solved, masked_row, precision=highest)  12.1 us
    dot_general x4, matrix products, apply_solve(): jnp.einsum('rbk,bjk->brj', blocked, inverse, preferred_element_type=jnp.f...  7.21 us

commit v1 on v0

v1 whole, which is shorter than its diff:
```python
import functools

import jax
import jax.numpy as jnp
from jax import lax
from jax.experimental import pallas as pl
from jax.experimental.pallas import tpu as pltpu
from jax.sharding import PartitionSpec as P

MESH = pl.DeviceIdType.MESH
LANES = 128
f32, bf16 = jnp.float32, jnp.bfloat16


def split(x):
    hi = x.astype(bf16)
    return hi, (x - hi.astype(f32)).astype(bf16)


def dot(a, b):
    return jnp.dot(a, b, preferred_element_type=f32)


def dot_nt(a, b):
    return lax.dot_general(a, b, (((1,), (1,)), ((), ())), preferred_element_type=f32)


def dot_split(a, b_hi, b_lo):
    a_hi, a_lo = split(a)
    rows = a.shape[0]
    both = dot(jnp.concatenate([a_hi, a_lo], axis=0), b_hi)
    return both[:rows] + both[rows:] + dot(a_hi, b_lo)


def dot_full(a, b):
    return dot_split(a, *split(b))


def each(count, body):
    if count <= 8:
        for i in range(count):
            body(i)
    else:
        lax.fori_loop(0, count, lambda i, c: (body(i), c)[1], 0)


def kernel(
    R, nb, bs, w, n,
    rhs, linv_h, llt, lrt, uinv_h, ult, urt, ranks,
    first, second,
    inv, ctp, ntp, wst, hs, got1, got2, send1, send2, g, table, y,
    load_sem, send_sem, recv_sem,
):
    me = lax.axis_index("rows")
    group = LANES // w
    quads = nb // group
    half = n // 2

    loads = []
    for f, src in ((0, linv_h), (1, uinv_h)):
        cp = pltpu.make_async_copy(src, inv.at[f], load_sem.at[f])
        cp.start()
        loads.append(cp)

    barrier = pltpu.get_barrier_semaphore()

    def greet(i):
        pl.semaphore_signal(
            barrier, inc=1, device_id={"rows": lax.rem(me + i + 1, R)}, device_id_type=MESH
        )

    each(R - 1, greet)

    ctp[...] = jnp.zeros_like(ctp)
    ntp[...] = jnp.zeros_like(ntp)

    lane = lax.broadcasted_iota(jnp.int32, (w, LANES), 1)
    row = lax.broadcasted_iota(jnp.int32, (w, LANES), 0)
    eye = (lax.rem(lane, w) == row).astype(f32)

    def lanes(rows):
        return lax.broadcasted_iota(jnp.int32, (rows, LANES), 1)

    def block(f, p):
        return p if f == 0 else nb - 1 - p

    lefts, rights = (llt, ult), (lrt, urt)
    kernels = ([], [])
    maps = [None, None]
    for f in (0, 1):
        loads[f].wait()
        wide_row = lax.broadcasted_iota(jnp.int32, (w, bs), 0)
        for p in range(nb):
            b = block(f, p)
            at = pl.ds(w * (p % group), w)
            ct = dot_nt(lefts[f][b], inv[f, b]).astype(bf16)
            ctp[f, p, at, :] = ct
            mt = jnp.where(wide_row < ranks[f, b], rights[f][b].astype(f32), 0.0).astype(bf16)
            hi, lo = split(dot(mt, inv[f, b]))
            ntp[f, 0, p, at, :] = hi
            ntp[f, 1, p, at, :] = lo
            kernels[f].append(eye - dot_nt(ct, jnp.concatenate([mt] * group, axis=0)))

    running = [eye, eye]
    columns = ([], [])
    for p in range(nb):
        for f in (0, 1):
            columns[f].append(running[f])
            moved = dot_full(running[f][:, :w], kernels[f][p])
            running[f] = jnp.concatenate([moved, eye], axis=0)

    full = w * (nb + 1)
    for f in (0, 1):
        maps[f] = running[f][:w]
        hi, lo = split(running[f][w:])
        wst[f, 0, quads] = hi
        wst[f, 1, quads] = lo
        for q in range(quads):
            total = jnp.zeros((full, LANES), f32)
            for k in range(group):
                col = columns[f][q * group + k]
                grown = jnp.concatenate([col, jnp.zeros((full - col.shape[0], LANES), f32)], axis=0)
                total = jnp.where(lanes(full) // w == k, grown, total)
            hi, lo = split(total[w:])
            wst[f, 0, q] = hi
            wst[f, 1, q] = lo
            p_hi, p_lo = split(total[:w])
            lhs = jnp.concatenate([p_hi, p_lo], axis=0)
            for k in range(group):
                p = q * group + k
                b = block(f, p)
                both = dot(lhs, ctp[f, p])
                hi, lo = split(both[:w] + both[w:])
                hs[f, :, b * bs : (b + 1) * bs] = jnp.concatenate([hi, hi, lo, lo], axis=0)

    def pushes(f, piece):
        parts = []
        for q in range(quads):
            total = None
            for k in range(group):
                p = q * group + k
                v = piece(block(f, p))
                term = dot_nt(v, ntp[f, 0, p]) + dot_nt(v, ntp[f, 1, p])
                total = term if total is None else total + term
            parts.append(total)
        return jnp.concatenate(parts, axis=1)

    def message(f, u):
        return dot_split(u, wst[f, 0, quads], wst[f, 1, quads])

    def local_blocks(f, piece, u):
        out = {}
        for q in range(quads):
            x_hi, x_lo = split(dot_split(u, wst[f, 0, q], wst[f, 1, q]))
            lhs = jnp.concatenate([x_hi, x_lo], axis=0)
            for k in range(group):
                p = q * group + k
                b = block(f, p)
                both = dot(lhs, ctp[f, p])
                out[b] = dot_nt(piece(b), inv[f, b]) - both[:n] - both[n:]
        return out

    def cols(b):
        return slice(b * bs, (b + 1) * bs)

    def fold(m, z):
        mixed = jnp.where(lax.rem(lanes(n) // w, 2) == 0, m, z)
        return jnp.where(lanes(half) < LANES // 2, mixed[:half], mixed[half:])

    def unfold(x):
        low = lanes(half) < LANES // 2
        return jnp.concatenate([jnp.where(low, x, 0.0), jnp.where(low, 0.0, x)], axis=0)

    def copy(k, src, dst, i):
        peer = lax.rem(me + i + 1, R)
        return pltpu.make_async_remote_copy(
            src_ref=src, dst_ref=dst.at[me], send_sem=send_sem.at[k, i],
            recv_sem=recv_sem.at[k, me], device_id={"rows": peer}, device_id_type=MESH,
        )

    def arrive(k, src, dst, i):
        peer = lax.rem(me + i + 1, R)
        pltpu.make_async_remote_copy(
            src_ref=src, dst_ref=dst.at[peer], send_sem=send_sem.at[k, i],
            recv_sem=recv_sem.at[k, peer], device_id={"rows": peer}, device_id_type=MESH,
        ).wait_recv()

    def sweep_start(piece):
        u = pushes(0, piece)
        m = message(0, u)
        out = local_blocks(0, piece, u)
        for b in range(nb):
            y[:, cols(b)] = out[b]
        return m

    def incoming(arrived):
        a = jnp.concatenate([unfold(arrived(e)) for e in range(R)], axis=1)
        a_hi, a_lo = split(a)
        both = jnp.concatenate([a_hi, a_lo], axis=0)
        states = []
        for k in (0, 1):
            r = dot(both, table[k, 0])
            s_hi, s_lo = split(r[:n] + r[n:] + dot(a_hi, table[k, 1]))
            even = lax.rem(lanes(n) // w, 2) == 0
            states.append(jnp.where(even, s_hi.astype(f32), s_lo.astype(f32)).astype(bf16))
        return states

    def sweep_end(s_f, s_b, out_ref):
        forward = [
            (y[:, cols(b)] - dot(s_f, hs[0, :, cols(b)])).astype(bf16) for b in range(nb)
        ]
        piece = lambda b: forward[b]
        u = pushes(1, piece)
        out = local_blocks(1, piece, u)
        for b in range(nb):
            out_ref[:, cols(b)] = out[b] - dot(s_b, hs[1, :, cols(b)])

    m = sweep_start(lambda b: rhs[:, cols(b)])
    mixed = pushes(
        1,
        lambda b: jnp.concatenate(
            [*split(y[:, cols(b)]), hs[0, :w, cols(b)], hs[0, 2 * w : 3 * w, cols(b)]], axis=0
        ),
    )
    u = jnp.concatenate(
        [mixed[:n] + mixed[n : 2 * n], mixed[2 * n : 2 * n + w] + mixed[2 * n + w :]], axis=0
    )
    zm = message(1, u)
    send1[:w] = jnp.where(
        lane < w, maps[0], jnp.where(lane < 2 * w, maps[1], jnp.where(lane < 3 * w, zm[n:], 0.0))
    )
    send1[w:] = fold(m, zm[:n])
    pl.semaphore_wait(barrier, R - 1)
    each(R - 1, lambda i: copy(0, send1, got1, i).start())
    got1[me] = send1[...]
    each(R - 1, lambda i: arrive(0, send1, got1, i))

    def mapped(e, k, v):
        t = jnp.where(lane // w == k, got1[e, :w], 0.0)
        return dot_full(t, jnp.concatenate([v] * group, axis=0))

    zero = jnp.zeros((w, LANES), f32)
    g[0, R - 1] = zero
    g[1, 0] = zero
    g[2, R - 1] = zero

    def chains(i):
        d = i
        g[1, d + 1] = mapped(d, 1, g[1, d]) + jnp.where(me == d, eye, 0.0)
        d = R - 1 - i
        g[0, d - 1] = mapped(d, 0, g[0, d]) + jnp.where(me == d, eye, 0.0)

    each(R - 1, chains)

    def cross(i):
        d = R - 1 - i
        g[2, d - 1] = mapped(d, 0, g[2, d]) + mapped(d, 2, g[1, d])

    each(R - 1, cross)

    def fill(e):
        at = pl.ds(e * LANES if isinstance(e, int) else pl.multiple_of(e * LANES, LANES), LANES)
        hi, lo = split(jnp.concatenate([g[0, e], zero] * 2, axis=0))
        table[0, 0, at] = hi
        table[0, 1, at] = lo
        hi, lo = split(jnp.concatenate([-g[2, e], g[1, e]] * 2, axis=0))
        table[1, 0, at] = hi
        table[1, 1, at] = lo

    each(R, fill)

    s_f, s_b = incoming(lambda e: got1[e, w:])
    sweep_end(s_f, s_b, first)

    m = sweep_start(lambda b: first[:, cols(b)].astype(bf16))
    mixed = pushes(1, lambda b: jnp.concatenate(split(y[:, cols(b)]), axis=0))
    z = message(1, mixed[:n] + mixed[n:])
    send2[...] = fold(m, z)
    each(R - 1, lambda i: copy(1, send2, got2, i).start())
    got2[me] = send2[...]
    each(R - 1, lambda i: arrive(1, send2, got2, i))
    s_f, s_b = incoming(lambda e: got2[e])
    sweep_end(s_f, s_b, second)

    each(R - 1, lambda i: copy(0, send1, got1, i).wait_send())
    each(R - 1, lambda i: copy(1, send2, got2, i).wait_send())


def local(R, rhs, linv, lleft, lright, uinv, uleft, uright, ranks):
    nb, bs, w = lleft.shape
    n = rhs.shape[0]
    flip = lambda a: jnp.swapaxes(a, 1, 2)
    vmem = pl.BlockSpec(memory_space=pltpu.VMEM)
    hbm = pl.BlockSpec(memory_space=pl.ANY)
    smem = pl.BlockSpec(memory_space=pltpu.SMEM)
    quads = nb * w // LANES
    out = jax.ShapeDtypeStruct(rhs.shape, f32)
    packed = w + n // 2
    return pl.pallas_call(
        functools.partial(kernel, R, nb, bs, w, n),
        out_shape=(out, out),
        in_specs=[vmem, hbm, vmem, vmem, hbm, vmem, vmem, smem],
        out_specs=(vmem, vmem),
        scratch_shapes=[
            pltpu.VMEM((2, nb, bs, bs), bf16),
            pltpu.VMEM((2, nb, LANES, bs), bf16),
            pltpu.VMEM((2, 2, nb, LANES, bs), bf16),
            pltpu.VMEM((2, 2, quads + 1, nb * w, LANES), bf16),
            pltpu.VMEM((2, 4 * w, nb * bs), bf16),
            pltpu.VMEM((R, packed, LANES), f32),
            pltpu.VMEM((R, n // 2, LANES), f32),
            pltpu.VMEM((packed, LANES), f32),
            pltpu.VMEM((n // 2, LANES), f32),
            pltpu.VMEM((3, R, w, LANES), f32),
            pltpu.VMEM((2, 2, R * LANES, LANES), bf16),
            pltpu.VMEM((n, nb * bs), f32),
            pltpu.SemaphoreType.DMA((2,)),
            pltpu.SemaphoreType.DMA((2, R)),
            pltpu.SemaphoreType.DMA((2, R)),
        ],
        compiler_params=pltpu.CompilerParams(
            collective_id=0, has_side_effects=True, vmem_limit_bytes=48 * 1024 * 1024
        ),
    )(rhs, linv, flip(lleft), flip(lright), uinv, flip(uleft), flip(uright), ranks)


def solution(mesh):
    blocks = P("rows", None, None)
    placed = (P("rhs", "rows"),) + (blocks,) * 6 + (P(None, "rows"),)
    return jax.shard_map(
        functools.partial(local, mesh.shape["rows"]),
        mesh=mesh,
        in_specs=placed,
        out_specs=(P("rhs", "rows"), P("rhs", "rows")),
        check_vma=False,
    )
```

time: 329 us -> 34.1 us (0.10); the launches traced: 325 us -> 33.8 us
  blocking collectives: 185 us -> 0 us
  matrix products: 104 us -> 0 us
  Pallas kernels: 0 us -> 24.2 us
  local copies, waits for them, and re-layouts: 25.2 us -> 8.89 us
  other arithmetic: 6.41 us -> 0 us
    all_gather x6 -> x0, blocking collectives: 185 us -> none  [the longest x4 122 us: carry_in(): lax.all_gather(offset[None], 'rows', axis=0, tiled=True)]
    dot_general x170 -> x0, matrix products: 104 us -> none  [the longest x64 73.3 us: local_advance(): solved = pushed_row - jnp.dot(state, coupled_row.T, precision=highest)]
    pallas_call x0 -> x1, Pallas kernels: none -> 24.2 us  [local(): pl.pallas_call(functools.partial(kernel, R, nb, bs, w, n), out_shape=(out...]
    unnamed x70 -> x18, local copies, waits for them, and re-layouts: 17.5 us -> 8.89 us
    pad x8 -> x0, local copies, waits for them, and re-layouts: 3.94 us -> none  [fold_collected(): folded = lax.associative_scan(compose_batched, (maps, offsets))]
where the time goes in v1:
time: 34.1 us; the launch traced here: 33.8 us
  Pallas kernels  24.2 us (71%)
  local copies, waits for them, and re-layouts  8.89 us (26%)
  between operations  0.66 us (2%)
    pallas_call x1, Pallas kernels, local(): pl.pallas_call(functools.partial(kernel, R, nb, bs, w, n), out_shape=(out...  24.2 us
    unnamed x18, local copies, waits for them, and re-layouts  8.89 us

profile of v1, /device:TPU:0, one launch (start us, length us, event | category | flops | bytes accessed | tf_op | source)
XLA Modules:
  0.0 33.8 jit_solution(14514328215849249672)
XLA Ops:
  0.6 0.0 copy-start.7
  0.6 0.7 %copy-done.7 = s32[2,8]{1,0:T(2,128)S(1)} copy-done((s32[2,8]{1,0:T(2,128)S(1)}, s32[2,8]{1,0:T(2,128)}, u32[]{:S(2)}) %copy-start.7) | copy-done | bytes 88
  1.3 0.0 copy-start
  1.3 1.2 %copy-done = bf16[8,256,256]{2,1,0:T(8,128)(2,1)S(1)} copy-done((bf16[8,256,256]{2,1,0:T(8,128)(2,1)S(1)}, bf16[8,256,256]{2,1,0:T(8,128)(2,1)}, u32[]{:S(2)}) %copy-start) | copy-done | bytes 1048600
  2.5 0.0 copy-start.1
  2.5 1.2 %copy-done.1 = bf16[8,256,256]{2,1,0:T(8,128)(2,1)S(1)} copy-done((bf16[8,256,256]{2,1,0:T(8,128)(2,1)S(1)}, bf16[8,256,256]{2,1,0:T(8,128)(2,1)}, u32[]{:S(2)}) %copy-start.1) | copy-done | bytes 1048600
  3.8 0.0 copy-start.2
  3.8 0.9 %copy-done.2 = bf16[8,256,32]{1,2,0:T(8,128)(2,1)S(1)} copy-done((bf16[8,256,32]{1,2,0:T(8,128)(2,1)S(1)}, bf16[8,256,32]{1,2,0:T(8,128)(2,1)}, u32[]{:S(2)}) %copy-start.2) | copy-done | bytes 131096
  4.7 0.0 copy-start.3
  4.7 0.9 %copy-done.3 = bf16[8,256,32]{1,2,0:T(8,128)(2,1)S(1)} copy-done((bf16[8,256,32]{1,2,0:T(8,128)(2,1)S(1)}, bf16[8,256,32]{1,2,0:T(8,128)(2,1)}, u32[]{:S(2)}) %copy-start.3) | copy-done | bytes 131096
  5.6 0.0 copy-start.4
  5.6 0.9 %copy-done.4 = bf16[8,256,32]{1,2,0:T(8,128)(2,1)S(1)} copy-done((bf16[8,256,32]{1,2,0:T(8,128)(2,1)S(1)}, bf16[8,256,32]{1,2,0:T(8,128)(2,1)}, u32[]{:S(2)}) %copy-start.4) | copy-done | bytes 131096
  6.5 0.0 copy-start.5
  6.5 0.9 %copy-done.5 = bf16[8,256,32]{1,2,0:T(8,128)(2,1)S(1)} copy-done((bf16[8,256,32]{1,2,0:T(8,128)(2,1)S(1)}, bf16[8,256,32]{1,2,0:T(8,128)(2,1)}, u32[]{:S(2)}) %copy-start.5) | copy-done | bytes 131096
  7.4 0.0 copy-start.6
  7.4 0.8 %copy-done.6 = bf16[16,2048]{1,0:T(8,128)(2,1)S(1)} copy-done((bf16[16,2048]{1,0:T(8,128)(2,1)S(1)}, bf16[16,2048]{1,0:T(8,128)(2,1)}, u32[]{:S(2)}) %copy-start.6) | copy-done | bytes 65560
  8.2 24.2 %shard_map.95 = (f32[16,2048]{1,0:T(8,128)S(1)}, f32[16,2048]{1,0:T(8,128)S(1)}) custom-call(bf16[16,2048]{1,0:T(8,128)(2,1)S(1)} %copy-done.6, bf16[8,256,256]{2,1,0:T(8,128)(2,1)S(1)} %copy-done, bf16[8,32,256]{2,1,0:T(8,128)(2,1)S(1)} %bitcast.4, bf16[8,32,256]{2,1,0:T(8,128)(2,1)S(1)} %bitcast.5, bf16[8,256,256]{2,1,0:T(8,128)(2,1)S(1)} %copy-done.1, ...), custom_call_target="tpu_custom_call" | custom-call | tf_op jit(solution)/shard_map/pallas_call | solution.py:299
  32.5 0.7 %copy.12 = f32[16,2048]{1,0:T(8,128)} copy(f32[16,2048]{1,0:T(8,128)S(1)} %get-tuple-element.4) | data formatting | bytes 262144
  33.1 0.7 %copy.13 = f32[16,2048]{1,0:T(8,128)} copy(f32[16,2048]{1,0:T(8,128)S(1)} %get-tuple-element.5) | data formatting | bytes 262144
Async XLA Ops:
  0.6 0.7 %copy-start.7 = (s32[2,8]{1,0:T(2,128)S(1)}, s32[2,8]{1,0:T(2,128)}, u32[]{:S(2)}) copy-start(s32[2,8]{1,0:T(2,128)} %ranks.1) | copy-start | bytes 196
  1.3 1.2 %copy-start = (bf16[8,256,256]{2,1,0:T(8,128)(2,1)S(1)}, bf16[8,256,256]{2,1,0:T(8,128)(2,1)}, u32[]{:S(2)}) copy-start(bf16[8,256,256]{2,1,0:T(8,128)(2,1)} %linv_h.1) | copy-start | bytes 3145732
  2.5 1.2 %copy-start.1 = (bf16[8,256,256]{2,1,0:T(8,128)(2,1)S(1)}, bf16[8,256,256]{2,1,0:T(8,128)(2,1)}, u32[]{:S(2)}) copy-start(bf16[8,256,256]{2,1,0:T(8,128)(2,1)} %uinv_h.1) | copy-start | bytes 3145732
  3.8 0.9 %copy-start.2 = (bf16[8,256,32]{1,2,0:T(8,128)(2,1)S(1)}, bf16[8,256,32]{1,2,0:T(8,128)(2,1)}, u32[]{:S(2)}) copy-start(bf16[8,256,32]{1,2,0:T(8,128)(2,1)} %param.10) | copy-start | bytes 393220
  4.7 0.9 %copy-start.3 = (bf16[8,256,32]{1,2,0:T(8,128)(2,1)S(1)}, bf16[8,256,32]{1,2,0:T(8,128)(2,1)}, u32[]{:S(2)}) copy-start(bf16[8,256,32]{1,2,0:T(8,128)(2,1)} %param.11) | copy-start | bytes 393220
  5.6 0.9 %copy-start.4 = (bf16[8,256,32]{1,2,0:T(8,128)(2,1)S(1)}, bf16[8,256,32]{1,2,0:T(8,128)(2,1)}, u32[]{:S(2)}) copy-start(bf16[8,256,32]{1,2,0:T(8,128)(2,1)} %param.13) | copy-start | bytes 393220
  6.5 0.9 %copy-start.5 = (bf16[8,256,32]{1,2,0:T(8,128)(2,1)S(1)}, bf16[8,256,32]{1,2,0:T(8,128)(2,1)}, u32[]{:S(2)}) copy-start(bf16[8,256,32]{1,2,0:T(8,128)(2,1)} %param.14) | copy-start | bytes 393220
  7.4 0.8 %copy-start.6 = (bf16[16,2048]{1,0:T(8,128)(2,1)S(1)}, bf16[16,2048]{1,0:T(8,128)(2,1)}, u32[]{:S(2)}) copy-start(bf16[16,2048]{1,0:T(8,128)(2,1)} %rhs.1) | copy-start | bytes 196612

commit v2 on v1

--- a/solution.py
+++ b/solution.py
@@ -36,6 +36,12 @@
     return dot_split(a, *split(b))
 
 
+def grow(x, rows):
+    if x.shape[0] == rows:
+        return x
+    return jnp.concatenate([x, jnp.zeros((rows - x.shape[0], LANES), f32)], axis=0)
+
+
 def each(count, body):
     if count <= 8:
         for i in range(count):
@@ -46,21 +52,32 @@
 
 def kernel(
     R, nb, bs, w, n,
-    rhs, linv_h, llt, lrt, uinv_h, ult, urt, ranks,
+    rhs_h, linv_h, llt_h, lrt_h, uinv_h, ult_h, urt_h, ranks_h,
     first, second,
-    inv, ctp, ntp, wst, hs, got1, got2, send1, send2, g, table, y,
-    load_sem, send_sem, recv_sem,
+    rhs, llt, lrt, ult, urt, ranks,
+    inv, ctp, ntp, wst, hs, got0, got1, got2, send0, send1, send2, g, walk, table, y,
+    load_sem, block_sem, send_sem, recv_sem,
 ):
     me = lax.axis_index("rows")
     group = LANES // w
     quads = nb // group
     half = n // 2
 
-    loads = []
-    for f, src in ((0, linv_h), (1, uinv_h)):
-        cp = pltpu.make_async_copy(src, inv.at[f], load_sem.at[f])
+    small = [
+        pltpu.make_async_copy(src, dst, load_sem.at[i])
+        for i, (src, dst) in enumerate(
+            ((llt_h, llt), (lrt_h, lrt), (ranks_h, ranks), (ult_h, ult), (urt_h, urt), (rhs_h, rhs))
+        )
+    ]
+    large = [
+        [
+            pltpu.make_async_copy(src.at[b], inv.at[f, b], block_sem.at[f, b])
+            for b in (range(nb) if f == 0 else reversed(range(nb)))
+        ]
+        for f, src in ((0, linv_h), (1, uinv_h))
+    ]
+    for cp in small[:3] + large[0] + small[3:5] + large[1] + small[5:]:
         cp.start()
-        loads.append(cp)
 
     barrier = pltpu.get_barrier_semaphore()
 
@@ -88,10 +105,12 @@
     kernels = ([], [])
     maps = [None, None]
     for f in (0, 1):
-        loads[f].wait()
+        for cp in small[:3] if f == 0 else small[3:5]:
+            cp.wait()
         wide_row = lax.broadcasted_iota(jnp.int32, (w, bs), 0)
         for p in range(nb):
             b = block(f, p)
+            large[f][p].wait()
             at = pl.ds(w * (p % group), w)
             ct = dot_nt(lefts[f][b], inv[f, b]).astype(bf16)
             ctp[f, p, at, :] = ct
@@ -101,26 +120,77 @@
             ntp[f, 1, p, at, :] = lo
             kernels[f].append(eye - dot_nt(ct, jnp.concatenate([mt] * group, axis=0)))
 
-    running = [eye, eye]
-    columns = ([], [])
-    for p in range(nb):
+    chains = {}
+    for q in range(quads):
         for f in (0, 1):
-            columns[f].append(running[f])
-            moved = dot_full(running[f][:, :w], kernels[f][p])
-            running[f] = jnp.concatenate([moved, eye], axis=0)
+            chains[f, q] = [eye]
+    for k in range(group):
+        for q in range(quads):
+            for f in (0, 1):
+                last = chains[f, q][-1]
+                moved = dot_full(last[:, :w], kernels[f][q * group + k])
+                chains[f, q].append(jnp.concatenate([moved, eye], axis=0))
 
     full = w * (nb + 1)
+    joined = {}
     for f in (0, 1):
-        maps[f] = running[f][:w]
-        hi, lo = split(running[f][w:])
+        before = None
+        for q in range(quads):
+            grown = w * (group + 1)
+            total = jnp.zeros((grown, LANES), f32)
+            for k in range(group):
+                col = chains[f, q][k]
+                total = jnp.where(lanes(grown) // w == k, grow(col, grown), total)
+            end = chains[f, q][group]
+            if before is not None:
+                moved = dot_full(before[:, :w], jnp.concatenate([total[:w], end[:w]], axis=1))
+                total = jnp.concatenate([moved[:, :LANES], total[w:]], axis=0)
+                end = jnp.concatenate([moved[:, LANES:], end[w:]], axis=0)
+            joined[f, q] = grow(total, full)
+            before = end
+        maps[f] = before[:w]
+        hi, lo = split(before[w:])
         wst[f, 0, quads] = hi
         wst[f, 1, quads] = lo
+
+    narrow = w // group
+    narrow_lanes = lanes(narrow) // w
+
+    def fold_map(x):
+        out = x[:narrow]
+        for k in range(1, group):
+            out = jnp.where(narrow_lanes == k, x[k * narrow : (k + 1) * narrow], out)
+        return out
+
+    def tile(x):
+        return jnp.concatenate([x] * group, axis=0)
+
+    def expand(x):
+        return jnp.where(lane // w == row // narrow, tile(x), 0.0)
+
+    def copy(k, src, dst, i):
+        peer = lax.rem(me + i + 1, R)
+        return pltpu.make_async_remote_copy(
+            src_ref=src, dst_ref=dst.at[me], send_sem=send_sem.at[k, i],
+            recv_sem=recv_sem.at[k, me], device_id={"rows": peer}, device_id_type=MESH,
+        )
+
+    def arrive(k, src, dst, i):
+        peer = lax.rem(me + i + 1, R)
+        pltpu.make_async_remote_copy(
+            src_ref=src, dst_ref=dst.at[peer], send_sem=send_sem.at[k, i],
+            recv_sem=recv_sem.at[k, peer], device_id={"rows": peer}, device_id_type=MESH,
+        ).wait_recv()
+
+    send0[:narrow] = fold_map(maps[0])
+    send0[narrow:] = fold_map(maps[1])
+    pl.semaphore_wait(barrier, R - 1)
+    each(R - 1, lambda i: copy(0, send0, got0, i).start())
+    got0[me] = send0[...]
+
+    for f in (0, 1):
         for q in range(quads):
-            total = jnp.zeros((full, LANES), f32)
-            for k in range(group):
-                col = columns[f][q * group + k]
-                grown = jnp.concatenate([col, jnp.zeros((full - col.shape[0], LANES), f32)], axis=0)
-                total = jnp.where(lanes(full) // w == k, grown, total)
+            total = joined[f, q]
             hi, lo = split(total[w:])
             wst[f, 0, q] = hi
             wst[f, 1, q] = lo
@@ -171,20 +241,6 @@
         low = lanes(half) < LANES // 2
         return jnp.concatenate([jnp.where(low, x, 0.0), jnp.where(low, 0.0, x)], axis=0)
 
-    def copy(k, src, dst, i):
-        peer = lax.rem(me + i + 1, R)
-        return pltpu.make_async_remote_copy(
-            src_ref=src, dst_ref=dst.at[me], send_sem=send_sem.at[k, i],
-            recv_sem=recv_sem.at[k, me], device_id={"rows": peer}, device_id_type=MESH,
-        )
-
-    def arrive(k, src, dst, i):
-        peer = lax.rem(me + i + 1, R)
-        pltpu.make_async_remote_copy(
-            src_ref=src, dst_ref=dst.at[peer], send_sem=send_sem.at[k, i],
-            recv_sem=recv_sem.at[k, peer], device_id={"rows": peer}, device_id_type=MESH,
-        ).wait_recv()
-
     def sweep_start(piece):
         u = pushes(0, piece)
         m = message(0, u)
@@ -215,6 +271,7 @@
         for b in range(nb):
             out_ref[:, cols(b)] = out[b] - dot(s_b, hs[1, :, cols(b)])
 
+    small[5].wait()
     m = sweep_start(lambda b: rhs[:, cols(b)])
     mixed = pushes(
         1,
@@ -226,64 +283,94 @@
         [mixed[:n] + mixed[n : 2 * n], mixed[2 * n : 2 * n + w] + mixed[2 * n + w :]], axis=0
     )
     zm = message(1, u)
-    send1[:w] = jnp.where(
-        lane < w, maps[0], jnp.where(lane < 2 * w, maps[1], jnp.where(lane < 3 * w, zm[n:], 0.0))
-    )
-    send1[w:] = fold(m, zm[:n])
-    pl.semaphore_wait(barrier, R - 1)
-    each(R - 1, lambda i: copy(0, send1, got1, i).start())
+    send1[:narrow] = fold_map(zm[n:])
+    send1[narrow:] = fold(m, zm[:n])
+    each(R - 1, lambda i: copy(1, send1, got1, i).start())
     got1[me] = send1[...]
-    each(R - 1, lambda i: arrive(0, send1, got1, i))
-
-    def mapped(e, k, v):
-        t = jnp.where(lane // w == k, got1[e, :w], 0.0)
-        return dot_full(t, jnp.concatenate([v] * group, axis=0))
 
     zero = jnp.zeros((w, LANES), f32)
-    g[0, R - 1] = zero
-    g[1, 0] = zero
-    g[2, R - 1] = zero
-
-    def chains(i):
-        d = i
-        g[1, d + 1] = mapped(d, 1, g[1, d]) + jnp.where(me == d, eye, 0.0)
-        d = R - 1 - i
-        g[0, d - 1] = mapped(d, 0, g[0, d]) + jnp.where(me == d, eye, 0.0)
-
-    each(R - 1, chains)
-
-    def cross(i):
-        d = R - 1 - i
-        g[2, d - 1] = mapped(d, 0, g[2, d]) + mapped(d, 2, g[1, d])
-
-    each(R - 1, cross)
+    spot = jnp.where(lane < w, eye, 0.0)
+    each(R - 1, lambda i: arrive(0, send0, got0, i))
+    g[1, 0:w] = zero
+
+    def rows_of(d):
+        return pl.ds(d * w if isinstance(d, int) else pl.multiple_of(d * w, w), w)
+
+    def backward_map(d):
+        moved = dot_full(expand(got0[d, narrow:]), tile(g[1, rows_of(d)]))
+        g[1, rows_of(d + 1)] = moved + jnp.where(me == d, eye, 0.0)
+
+    def forward_map(d, state):
+        return dot_full(state, tile(expand(got0[d, :narrow])))
+
+    def crossed(d, state):
+        return dot_full(
+            dot_full(state, tile(expand(got1[d, :narrow]))), tile(g[1, rows_of(d)])
+        )
+
+    if R <= 8:
+        history = [None]
+        for d in range(R - 1):
+            backward_map(d)
+            last = history[-1]
+            grown = spot if last is None else jnp.concatenate([forward_map(d, last), spot], axis=0)
+            history.append(grown)
+        chosen = jnp.zeros((R * w, LANES), f32)
+        for d in range(1, R):
+            chosen = jnp.where(me == d, grow(history[d], R * w), chosen)
+        g[0] = chosen
+        each(R - 1, lambda i: arrive(1, send1, got1, i))
+        total = jnp.zeros((R * w, LANES), f32)
+        for d in range(1, R):
+            total += grow(crossed(d, history[d]), R * w)
+        g[2] = total
+    else:
+        each(R - 1, backward_map)
+        each(R - 1, lambda i: arrive(1, send1, got1, i))
+        walk[...] = jnp.zeros_like(walk)
+        g[0] = jnp.zeros((R * w, LANES), f32)
+        g[2] = jnp.zeros((R * w, LANES), f32)
+
+        def step(d):
+            state = walk[...]
+            g[0] = jnp.where(me == d, state, g[0])
+            g[2] = g[2] + crossed(d, state)
+            walk[...] = forward_map(d, state)
+            walk[rows_of(d)] = spot
+
+        each(R, step)
+
+    c_hi, c_lo = split(g[0])
+    spread = tile(eye).astype(bf16)
+    g[0] = dot(c_hi, spread) + dot(c_lo, spread)
 
     def fill(e):
         at = pl.ds(e * LANES if isinstance(e, int) else pl.multiple_of(e * LANES, LANES), LANES)
-        hi, lo = split(jnp.concatenate([g[0, e], zero] * 2, axis=0))
+        hi, lo = split(jnp.concatenate([g[0, rows_of(e)], zero] * 2, axis=0))
         table[0, 0, at] = hi
         table[0, 1, at] = lo
-        hi, lo = split(jnp.concatenate([-g[2, e], g[1, e]] * 2, axis=0))
+        hi, lo = split(jnp.concatenate([-g[2, rows_of(e)], g[1, rows_of(e)]] * 2, axis=0))
         table[1, 0, at] = hi
         table[1, 1, at] = lo
 
     each(R, fill)
 
-    s_f, s_b = incoming(lambda e: got1[e, w:])
+    s_f, s_b = incoming(lambda e: got1[e, narrow:])
     sweep_end(s_f, s_b, first)
 
     m = sweep_start(lambda b: first[:, cols(b)].astype(bf16))
     mixed = pushes(1, lambda b: jnp.concatenate(split(y[:, cols(b)]), axis=0))
     z = message(1, mixed[:n] + mixed[n:])
     send2[...] = fold(m, z)
-    each(R - 1, lambda i: copy(1, send2, got2, i).start())
+    each(R - 1, lambda i: copy(2, send2, got2, i).start())
     got2[me] = send2[...]
-    each(R - 1, lambda i: arrive(1, send2, got2, i))
+    each(R - 1, lambda i: arrive(2, send2, got2, i))
     s_f, s_b = incoming(lambda e: got2[e])
     sweep_end(s_f, s_b, second)
 
-    each(R - 1, lambda i: copy(0, send1, got1, i).wait_send())
-    each(R - 1, lambda i: copy(1, send2, got2, i).wait_send())
+    each(R - 1, lambda i: copy(0, send0, got0, i).wait_send())
+    each(R - 1, lambda i: copy(1, send1, got1, i).wait_send())
+    each(R - 1, lambda i: copy(2, send2, got2, i).wait_send())
 
 
 def local(R, rhs, linv, lleft, lright, uinv, uleft, uright, ranks):
@@ -291,35 +378,43 @@
     n = rhs.shape[0]
     flip = lambda a: jnp.swapaxes(a, 1, 2)
     vmem = pl.BlockSpec(memory_space=pltpu.VMEM)
-    hbm = pl.BlockSpec(memory_space=pl.ANY)
-    smem = pl.BlockSpec(memory_space=pltpu.SMEM)
+    hbm = pl.BlockSpec(memory_space=pltpu.HBM)
     quads = nb * w // LANES
     out = jax.ShapeDtypeStruct(rhs.shape, f32)
-    packed = w + n // 2
+    narrow = w * w // LANES
+    packed = narrow + n // 2
+    slim = pltpu.VMEM((nb, w, bs), bf16)
     return pl.pallas_call(
         functools.partial(kernel, R, nb, bs, w, n),
         out_shape=(out, out),
-        in_specs=[vmem, hbm, vmem, vmem, hbm, vmem, vmem, smem],
+        in_specs=[hbm] * 8,
         out_specs=(vmem, vmem),
         scratch_shapes=[
+            pltpu.VMEM(rhs.shape, bf16),
+            slim, slim, slim, slim,
+            pltpu.SMEM(ranks.shape, jnp.int32),
             pltpu.VMEM((2, nb, bs, bs), bf16),
             pltpu.VMEM((2, nb, LANES, bs), bf16),
             pltpu.VMEM((2, 2, nb, LANES, bs), bf16),
             pltpu.VMEM((2, 2, quads + 1, nb * w, LANES), bf16),
             pltpu.VMEM((2, 4 * w, nb * bs), bf16),
+            pltpu.VMEM((R, 2 * narrow, LANES), f32),
             pltpu.VMEM((R, packed, LANES), f32),
             pltpu.VMEM((R, n // 2, LANES), f32),
+            pltpu.VMEM((2 * narrow, LANES), f32),
             pltpu.VMEM((packed, LANES), f32),
             pltpu.VMEM((n // 2, LANES), f32),
-            pltpu.VMEM((3, R, w, LANES), f32),
+            pltpu.VMEM((3, R * w, LANES), f32),
+            pltpu.VMEM((R * w, LANES), f32),
             pltpu.VMEM((2, 2, R * LANES, LANES), bf16),
             pltpu.VMEM((n, nb * bs), f32),
-            pltpu.SemaphoreType.DMA((2,)),
-            pltpu.SemaphoreType.DMA((2, R)),
-            pltpu.SemaphoreType.DMA((2, R)),
+            pltpu.SemaphoreType.DMA((6,)),
+            pltpu.SemaphoreType.DMA((2, nb)),
+            pltpu.SemaphoreType.DMA((3, R)),
+            pltpu.SemaphoreType.DMA((3, R)),
         ],
         compiler_params=pltpu.CompilerParams(
-            collective_id=0, has_side_effects=True, vmem_limit_bytes=48 * 1024 * 1024
+            collective_id=0, has_side_effects=True, vmem_limit_bytes=67043328
         ),
     )(rhs, linv, flip(lleft), flip(lright), uinv, flip(uleft), flip(uright), ranks)
 

time: 34.1 us -> 28.8 us (0.84)
  local copies, waits for them, and re-layouts: 8.89 us -> 2.26 us
  Pallas kernels: 24.2 us -> 25.7 us
    unnamed x18 -> x4, local copies, waits for them, and re-layouts: 8.89 us -> 2.26 us
    pallas_call x1, Pallas kernels: 24.2 us -> 25.7 us  [local(): pl.pallas_call(functools.partial(kernel, R, nb, bs, w, n), out_shape=(out...]
where the time goes in v2:
time: 28.8 us; the launch traced here: 28.7 us
  Pallas kernels  25.7 us (89%)
  local copies, waits for them, and re-layouts  2.26 us (8%)
  between operations  0.65 us (2%)
    pallas_call x1, Pallas kernels, local(): pl.pallas_call(functools.partial(kernel, R, nb, bs, w, n), out_shape=(out...  25.7 us
    unnamed x4, local copies, waits for them, and re-layouts  2.26 us

profile of v2, /device:TPU:0, one launch (start us, length us, event | category | flops | bytes accessed | tf_op | source)
XLA Modules:
  0.0 28.7 jit_solution(11492553986708118739)
XLA Ops:
  0.6 25.7 %shard_map.95 = (f32[16,2048]{1,0:T(8,128)}, f32[16,2048]{1,0:T(8,128)}) custom-call(bf16[16,2048]{1,0:T(8,128)(2,1)} %rhs_h.1, bf16[8,256,256]{2,1,0:T(8,128)(2,1)} %linv_h.1, bf16[8,32,256]{2,1,0:T(8,128)(2,1)} %bitcast.4, bf16[8,32,256]{2,1,0:T(8,128)(2,1)} %bitcast.5, bf16[8,256,256]{2,1,0:T(8,128)(2,1)} %uinv_h.1, bf16[8,32,256]{2,1,0:T(8,128)(2,1)} %bitcast.6, ...), custom_call_target="tpu_custom_call" | custom-call | tf_op jit(solution)/shard_map/pallas_call | solution.py:387
  26.4 0.0 copy-start
  26.4 1.6 %copy.12 = f32[16,2048]{1,0:T(8,128)} copy(f32[16,2048]{1,0:T(8,128)} %get-tuple-element.4) | data formatting | bytes 262144
  28.0 0.0 copy-done
  28.0 0.7 %copy.13 = f32[16,2048]{1,0:T(8,128)} copy(f32[16,2048]{1,0:T(8,128)S(1)} %copy-done) | data formatting | bytes 262144
Async XLA Ops:
  26.4 1.6 %copy-start = (f32[16,2048]{1,0:T(8,128)S(1)}, f32[16,2048]{1,0:T(8,128)}, u32[]{:S(2)}) copy-start(f32[16,2048]{1,0:T(8,128)} %get-tuple-element.5) | copy-start | bytes 393220
